TPU v7x, 256 devices: a whole 4x4x8 slice. The times are simulated.
256 devices in a mesh: grid: 16 (over y, x), mic: 4 (over z_hi), bin: 4 (over z_lo, core).
Axes of the slice: x: 4, y: 4, z: 8 (z_hi: 4, z_lo: 2; z = z_hi * 2 + z_lo), core: 2. Of those that a mesh axis runs over, the one named last changes fastest.
Arguments:
- grid_points: float32 [3, 16384], P(None, 'grid'), may hold values from -1 to 3, as said below
- mic_coords: float32 [3, 4096], P(None, 'mic'), may hold values from -1 to 1, as said below
- wavenumbers: float32 [16], P('bin'), may hold values from 20 to 150
- pressures: float32 [16, 2, 16, 4096], P('bin', None, None, 'mic'), may hold values from -6 to 6
Outputs:
- solution: float32 [16, 2, 16, 16384], P('bin', None, None, 'grid')
- residual: float32 [16, 2, 16, 4096], P('bin', None, None, 'mic')
Inputs may be any that keep to these rules, and one draw needn't show every extreme that they name: `grid_points`: rows 0 and 1 lie in -1 to 1, row 2 in 1 to 3. `mic_coords`: rows 0 and 1 lie in -1 to 1, row 2 in -0.05 to 0.05.
All inputs are finite; a program needn't handle non-finite values.
Results may differ from a plain program's by a relative error of at most 0.0055.
Values may be sent and summed in bfloat16 or wider, within the bound.
No kernel may reach another device: no remote copies, remote signals or barrier semaphores. Data moves between devices by JAX's collectives and lax.ppermute only.
A program may use at most 64 MiB of HBM per device.

v0:
```python
import math
import jax
import jax.numpy as jnp
from jax import lax
from jax.sharding import PartitionSpec as P

ITERS = 2


def steering_tiles(grid_points, mic_coords, wavenumbers, norm_scale):
    dist_x = grid_points[0][:, None] - mic_coords[0][None, :]
    dist_y = grid_points[1][:, None] - mic_coords[1][None, :]
    dist_z = grid_points[2][:, None] - mic_coords[2][None, :]
    radius = jnp.sqrt(dist_x * dist_x + dist_y * dist_y + dist_z * dist_z)
    amplitude = norm_scale / radius
    cos_list = []
    sin_list = []
    for bin_index in range(wavenumbers.shape[0]):
        phase_angle = wavenumbers[bin_index] * radius
        cos_list.append((jnp.cos(phase_angle) * amplitude).astype(jnp.bfloat16))
        sin_list.append((jnp.sin(phase_angle) * amplitude).astype(jnp.bfloat16))
    return (jnp.stack(cos_list), jnp.stack(sin_list))


def body(grid_points, mic_coords, wavenumbers, pressures):
    bin_count = pressures.shape[0]
    snap_count = pressures.shape[2]
    grid_local = grid_points.shape[1]
    norm_scale = 1.0 / math.sqrt(grid_local * lax.axis_size("grid"))
    cos_tiles, sin_tiles = steering_tiles(grid_points, mic_coords, wavenumbers, norm_scale)

    def combine_adjoint(cos_sum, sin_sum):
        real_part = cos_sum[:, :snap_count] - sin_sum[:, snap_count:]
        imag_part = cos_sum[:, snap_count:] + sin_sum[:, :snap_count]
        return jnp.stack([real_part, imag_part], axis=1)

    def apply_adjoint(residual):
        rounded = residual.astype(jnp.bfloat16).reshape(
            bin_count, 2 * snap_count, residual.shape[3]
        )
        cos_sum = jnp.einsum("fkm,fgm->fkg", rounded, cos_tiles, preferred_element_type=jnp.float32)
        sin_sum = jnp.einsum("fkm,fgm->fkg", rounded, sin_tiles, preferred_element_type=jnp.float32)
        partial_terms = combine_adjoint(cos_sum, sin_sum)
        summed = lax.psum(partial_terms, "mic")
        grad_norm = lax.psum(jnp.sum(summed * summed), ("grid", "bin"))
        return (summed, grad_norm)

    residual = pressures
    gradient, grad_norm = apply_adjoint(residual)
    direction = gradient
    solution = jnp.zeros_like(gradient)
    for iteration in range(ITERS):
        apply_rounded = direction.astype(jnp.bfloat16).reshape(
            bin_count, 2 * snap_count, direction.shape[3]
        )
        apply_cos_sum = jnp.einsum(
            "fkg,fgm->fkm", apply_rounded, cos_tiles, preferred_element_type=jnp.float32
        )
        apply_sin_sum = jnp.einsum(
            "fkg,fgm->fkm", apply_rounded, sin_tiles, preferred_element_type=jnp.float32
        )
        combine_real_part = apply_cos_sum[:, :snap_count] + apply_sin_sum[:, snap_count:]
        combine_imag_part = apply_cos_sum[:, snap_count:] - apply_sin_sum[:, :snap_count]
        apply_partial_terms = jnp.stack([combine_real_part, combine_imag_part], axis=1)
        apply_summed = lax.psum(apply_partial_terms, "grid")
        image_norm = lax.psum(jnp.sum(apply_summed * apply_summed), ("mic", "bin"))
        image, image_norm = (apply_summed, image_norm)
        step_size = grad_norm / image_norm
        solution = solution + step_size * direction
        residual = residual - step_size * image
        if iteration + 1 < ITERS:
            gradient, next_norm = apply_adjoint(residual)
            direction = gradient + next_norm / grad_norm * direction
            grad_norm = next_norm
    return (solution, residual)


def solution(mesh):
    placed = (P(None, "grid"), P(None, "mic"), P("bin"), P("bin", None, None, "mic"))
    return jax.shard_map(
        body,
        mesh=mesh,
        in_specs=placed,
        out_specs=(P("bin", None, None, "grid"), P("bin", None, None, "mic")),
        check_vma=False,
    )
```

profile of v0, /device:TPU:1, one launch (start us, length us, event | category | flops | bytes accessed | tf_op | source)
XLA Modules:
  0.0 768.9 jit_solution(6533060130410521625)
XLA Ops:
  7.2 0.0 all-reduce.5.cloned.1.call-start
  7.2 1.5 fusion.13
  8.7 0.8 fusion.11
  9.5 0.8 fusion.12
  10.4 1.1 convert_element_type.96
  11.5 67.4 %multiply_convert_fusion.7 = (bf16[1,1024,1024]{2,1,0:T(8,128)(2,1)S(1)}, bf16[1,1024,1024]{2,1,0:T(8,128)(2,1)S(1)}, bf16[1,1024,1024]{2,1,0:T(8,128)(2,1)S(1)}...) fusion(f32[1024]{0:T(1024)S(1)} %bitcast.62, ...), kind=kLoop, calls=%fused_computation.9 | loop fusion | flops 30408704 | bytes 16801808 | tf_op jit(solution)/shard_map/convert_element_type | solution.py:20
  78.9 2.4 pad_maximum_fusion
  81.3 0.0 copy-start
  81.3 0.0 copy-start.2
  81.3 2.6 convolution_bitcast_fusion
  83.9 0.6 copy-done
  84.5 2.5 copy-done.2
  87.0 2.6 convolution_bitcast_fusion.1
  89.6 0.1 fusion.8
  89.6 0.8 pad_maximum_fusion.2
  90.5 0.0 all-reduce.5.cloned.1.call-update
  90.5 0.0 all-reduce.7.cloned.1.call-start
  90.6 56.2 %all-reduce.5.cloned.1.call-done = f32[4,2,16,1024]{3,2,0,1:T(8,128)} async-done(((f32[4,2,16,1024]{3,2,0,1:T(8,128)}), f32[4,2,16,1024]{3,2,0,1:T(8,128)}) %all-reduce.5.cloned.1.call-update) | async-done | bytes 524304 | tf_op jit(solution)/shard_map/psum | solution.py:44
  146.7 1.9 multiply_reduce_fusion.3
  148.7 0.0 copy-start.1
  148.7 5.1 fusion.14
  153.8 0.7 copy-done.1
  154.5 0.0 copy-start.5
  154.5 1.5 fusion.15
  156.0 0.1 fusion.6
  156.1 0.8 pad_maximum_fusion.3
  156.9 0.0 all-reduce.7.cloned.1.call-update
  156.9 0.0 all-reduce.9.cloned.1.call-start
  157.0 94.4 %all-reduce.7.cloned.1.call-done = f32[4,2,16,1024]{3,2,0,1:T(8,128)} async-done(((f32[4,2,16,1024]{3,2,0,1:T(8,128)}), f32[4,2,16,1024]{3,2,0,1:T(8,128)}) %all-reduce.7.cloned.1.call-update) | async-done | bytes 524304 | tf_op jit(solution)/shard_map/psum | solution.py:65
  251.4 1.8 multiply_reduce_fusion.2
  253.2 140.4 %psum.57 = f32[]{:T(128)} all-reduce(f32[]{:T(128)} %get-tuple-element.14), channel_id=1, replica_groups=mesh['grid'=16,'mic'=4,'bin'=4] {'grid','bin'}, use_global_device_ids=true, to_apply=%region_2.0 | all-reduce | flops 1 | bytes 8 | tf_op jit(solution)/shard_map/psum | solution.py:45
  393.6 25.9 %psum.59 = f32[]{:T(128)} all-reduce(f32[]{:T(128)} %multiply_reduce_fusion.2), channel_id=1, replica_groups=mesh['grid'=16,'mic'=4,'bin'=4] {'mic','bin'}, use_global_device_ids=true, to_apply=%region_5.0 | all-reduce | flops 1 | bytes 8 | tf_op jit(solution)/shard_map/psum | solution.py:66
  420.8 0.0 copy-done.5
  420.8 1.1 fusion.10
  422.0 5.9 fusion.16
  427.9 0.0 copy-start.3
  427.9 6.0 fusion.17
  434.0 0.1 fusion.4
  434.0 0.8 pad_maximum_fusion.4
  434.9 0.0 all-reduce.9.cloned.1.call-update
  434.9 0.0 all-reduce.11.cloned.1.call-start
  434.9 47.9 %all-reduce.9.cloned.1.call-done = f32[4,2,16,1024]{3,2,0,1:T(8,128)} async-done(((f32[4,2,16,1024]{3,2,0,1:T(8,128)}), f32[4,2,16,1024]{3,2,0,1:T(8,128)}) %all-reduce.9.cloned.1.call-update) | async-done | bytes 524304 | tf_op jit(solution)/shard_map/psum | solution.py:44
  482.8 1.8 multiply_reduce_fusion.1
  484.6 140.7 %psum.61 = f32[]{:T(128)} all-reduce(f32[]{:T(128)} %multiply_reduce_fusion.1), channel_id=1, replica_groups=mesh['grid'=16,'mic'=4,'bin'=4] {'grid','bin'}, use_global_device_ids=true, to_apply=%region_8.0 | all-reduce | flops 1 | bytes 8 | tf_op jit(solution)/shard_map/psum | solution.py:45
  626.6 0.0 copy-done.3
  626.6 1.1 fusion.9
  627.8 4.9 fusion.18
  632.7 0.0 copy-start.6
  632.7 5.0 fusion.19
  637.7 0.0 copy-start.4
  637.7 0.1 fusion.2
  637.8 0.8 pad_maximum_fusion.5
  638.6 0.0 all-reduce.11.cloned.1.call-update
  638.6 91.7 %all-reduce.11.cloned.1.call-done = f32[4,2,16,1024]{3,2,0,1:T(8,128)} async-done(((f32[4,2,16,1024]{3,2,0,1:T(8,128)}), f32[4,2,16,1024]{3,2,0,1:T(8,128)}) %all-reduce.11.cloned.1.call-update) | async-done | bytes 524304 | tf_op jit(solution)/shard_map/psum | solution.py:65
  730.4 1.8 multiply_reduce_fusion
  732.1 26.0 %psum.63 = f32[]{:T(128)} all-reduce(f32[]{:T(128)} %multiply_reduce_fusion), channel_id=1, replica_groups=mesh['grid'=16,'mic'=4,'bin'=4] {'mic','bin'}, use_global_device_ids=true, to_apply=%region_11.0 | all-reduce | flops 1 | bytes 8 | tf_op jit(solution)/shard_map/psum | solution.py:66
  759.4 0.0 copy-done.6
  759.4 1.2 multiply_subtract_fusion
  760.6 0.8 copy.14
  761.5 0.0 copy-done.4
  761.5 0.1 multiply_add_fusion
  761.6 0.8 copy.13
  (3 shorter events, 0.1 us)
Async XLA Ops:
  7.2 139.6 %all-reduce.5.cloned.1.call-start = ((), (), s32[]{:S(2)}) async-start(), calls=%async_computation | async-start | bytes 1048576 | tf_op jit(solution)/shard_map/psum | solution.py:44
  81.3 3.2 copy-start
  81.3 5.7 copy-start.2
  90.5 160.9 %all-reduce.7.cloned.1.call-start = ((), (), s32[]{:S(2)}) async-start(), calls=%async_computation.1 | async-start | bytes 1048576 | tf_op jit(solution)/shard_map/psum | solution.py:65
  148.7 5.8 copy-start.1
  154.5 266.4 %copy-start.5 = (f32[4,2,16,1024]{3,2,1,0:T(8,128)S(1)}, f32[4,2,16,1024]{3,2,1,0:T(8,128)}, u32[]{:S(2)}) copy-start(f32[4,2,16,1024]{3,2,1,0:T(8,128)} %param.7) | copy-start | bytes 1572868
  156.9 325.9 %all-reduce.9.cloned.1.call-start = ((), (), s32[]{:S(2)}) async-start(), calls=%async_computation.2 | async-start | bytes 1048576 | tf_op jit(solution)/shard_map/psum | solution.py:44
  427.9 198.7 %copy-start.3 = (f32[4,2,16,1024]{3,2,0,1:T(8,128)S(1)}, f32[4,2,16,1024]{3,2,0,1:T(8,128)}, u32[]{:S(2)}) copy-start(f32[4,2,16,1024]{3,2,0,1:T(8,128)} %all-reduce.5.cloned.1.call-done) | copy-start | bytes 1572868
  434.9 295.5 %all-reduce.11.cloned.1.call-start = ((), (), s32[]{:S(2)}) async-start(), calls=%async_computation.3 | async-start | bytes 1048576 | tf_op jit(solution)/shard_map/psum | solution.py:65
  632.7 126.7 %copy-start.6 = (f32[4,2,16,1024]{3,2,0,1:T(8,128)S(1)}, f32[4,2,16,1024]{3,2,0,1:T(8,128)}, u32[]{:S(2)}) copy-start(f32[4,2,16,1024]{3,2,0,1:T(8,128)} %all-reduce.7.cloned.1.call-done) | copy-start | bytes 1572868
  637.7 123.8 %copy-start.4 = (f32[4,2,16,1024]{3,2,0,1:T(8,128)S(1)}, f32[4,2,16,1024]{3,2,0,1:T(8,128)}, u32[]{:S(2)}) copy-start(f32[4,2,16,1024]{3,2,0,1:T(8,128)} %all-reduce.9.cloned.1.call-done) | copy-start | bytes 1572868
Sparse Core Ops, SparseCore 0:
  90.6 56.0 all-reduce.4
  157.1 94.3 all-reduce.6
  435.0 47.7 all-reduce.8
  638.7 91.5 all-reduce.10
where the time goes:
time: 770 us; the launch traced here: 769 us
  blocking collectives  333 us (43%)
  waiting for transfers between devices  290 us (38%)
  other arithmetic  85.2 us (11%)
  matrix products  33.6 us (4%)
  between operations  17.9 us (2%)
  local copies, waits for them, and re-layouts  8.73 us (1%)
    psum x2, blocking collectives, apply_adjoint(): grad_norm = lax.psum(jnp.sum(summed * summed), ('grid', 'bin'))  281 us
    psum x2, waiting for transfers between devices, body(): apply_summed = lax.psum(apply_partial_terms, 'grid')  186 us
    psum x2, waiting for transfers between devices, apply_adjoint(): summed = lax.psum(partial_terms, 'mic')  104 us
    convert_element_type x1, other arithmetic, steering_tiles(): cos_list.append((jnp.cos(phase_angle) * amplitude).astype(jnp.bfloat16))  67.4 us
    psum x2, blocking collectives, body(): image_norm = lax.psum(jnp.sum(apply_summed * apply_summed), ('mic', 'bin'))  51.9 us
  transfers between devices with their start and end apart: 4, of which 4 were waited for; matrix products, arithmetic and copies ran while one was open for 0% of the time, Pallas kernels for 0%

commit v1 on v0

--- a/solution.py
+++ b/solution.py
@@ -5,6 +5,11 @@
 from jax.sharding import PartitionSpec as P
 
 ITERS = 2
+
+
+def add_all(x, axis):
+    shards = lax.all_gather(x, axis)
+    return jnp.sum(shards, axis=0)
 
 
 def steering_tiles(grid_points, mic_coords, wavenumbers, norm_scale):
@@ -62,7 +67,7 @@
         combine_real_part = apply_cos_sum[:, :snap_count] + apply_sin_sum[:, snap_count:]
         combine_imag_part = apply_cos_sum[:, snap_count:] - apply_sin_sum[:, :snap_count]
         apply_partial_terms = jnp.stack([combine_real_part, combine_imag_part], axis=1)
-        apply_summed = lax.psum(apply_partial_terms, "grid")
+        apply_summed = add_all(apply_partial_terms, "grid")
         image_norm = lax.psum(jnp.sum(apply_summed * apply_summed), ("mic", "bin"))
         image, image_norm = (apply_summed, image_norm)
         step_size = grad_norm / image_norm

time: 770 us -> 738 us (0.958)
  waiting for transfers between devices: 290 us -> 254 us
    psum x2 -> x0, waiting for transfers between devices: 186 us -> none  [body(): apply_summed = lax.psum(apply_partial_terms, 'grid')]
    all_gather x0 -> x2, waiting for transfers between devices: none -> 150 us  [add_all(): shards = lax.all_gather(x, axis)]
    reduce_sum x0 -> x2, other arithmetic: none -> 8.59 us  [add_all(): return jnp.sum(shards, axis=0)]
where the time goes in v1:
time: 738 us; the launch traced here: 736 us
  blocking collectives  332 us (45%)
  waiting for transfers between devices  254 us (34%)
  other arithmetic  89.8 us (12%)
  matrix products  33.5 us (5%)
  between operations  17.8 us (2%)
  local copies, waits for them, and re-layouts  8.73 us (1%)
    psum x2, blocking collectives, apply_adjoint(): grad_norm = lax.psum(jnp.sum(summed * summed), ('grid', 'bin'))  280 us
    all_gather x2, waiting for transfers between devices, add_all(): shards = lax.all_gather(x, axis)  150 us
    psum x2, waiting for transfers between devices, apply_adjoint(): summed = lax.psum(partial_terms, 'mic')  104 us
    convert_element_type x1, other arithmetic, steering_tiles(): cos_list.append((jnp.cos(phase_angle) * amplitude).astype(jnp.bfloat16))  67.5 us
    psum x2, blocking collectives, body(): image_norm = lax.psum(jnp.sum(apply_summed * apply_summed), ('mic', 'bin'))  52.2 us
  transfers between devices with their start and end apart: 4, of which 4 were waited for; matrix products, arithmetic and copies ran while one was open for 0% of the time, Pallas kernels for 0%

profile of v1, /device:TPU:1, one launch (start us, length us, event | category | flops | bytes accessed | tf_op | source)
XLA Modules:
  0.0 735.6 jit_solution(16639605374000150899)
XLA Ops:
  7.2 0.0 all-reduce.3.cloned.1.call-start
  7.2 1.5 fusion.13
  8.7 0.8 fusion.11
  9.5 0.8 fusion.12
  10.4 1.1 convert_element_type.96
  11.5 67.5 %multiply_convert_fusion.7 = (bf16[1,1024,1024]{2,1,0:T(8,128)(2,1)S(1)}, bf16[1,1024,1024]{2,1,0:T(8,128)(2,1)S(1)}, bf16[1,1024,1024]{2,1,0:T(8,128)(2,1)S(1)}...) fusion(f32[1024]{0:T(1024)S(1)} %bitcast.66, ...), kind=kLoop, calls=%fused_computation.9 | loop fusion | flops 30408704 | bytes 16801808 | tf_op jit(solution)/shard_map/convert_element_type | solution.py:25
  78.9 2.4 pad_maximum_fusion
  81.3 0.0 copy-start
  81.3 0.0 copy-start.2
  81.3 2.6 convolution_bitcast_fusion
  83.9 0.6 copy-done
  84.5 2.5 copy-done.2
  87.0 2.6 convolution_bitcast_fusion.1
  89.6 0.1 fusion.8
  89.7 0.8 pad_maximum_fusion.2
  90.5 0.0 all-reduce.3.cloned.1.call-update
  90.5 0.0 all-gather.5.cloned.1.call-start
  90.6 55.9 %all-reduce.3.cloned.1.call-done = f32[4,2,16,1024]{3,2,0,1:T(8,128)} async-done(((f32[4,2,16,1024]{3,2,0,1:T(8,128)}), f32[4,2,16,1024]{3,2,0,1:T(8,128)}) %all-reduce.3.cloned.1.call-update) | async-done | bytes 524304 | tf_op jit(solution)/shard_map/psum | solution.py:49
  146.5 2.0 multiply_reduce_fusion.3
  148.5 0.0 copy-start.1
  148.5 5.1 fusion.14
  153.6 0.7 copy-done.1
  154.3 1.5 fusion.15
  155.8 0.1 fusion.6
  155.9 0.8 pad_maximum_fusion.3
  156.8 0.0 all-gather.5.cloned.1.call-update
  156.8 0.0 all-reduce.5.cloned.1.call-start
  156.8 76.3 %all-gather.5.cloned.1.call-done = f32[64,2,16,1024]{3,2,0,1:T(8,128)} async-done(((f32[4,2,16,1024]{3,2,0,1:T(8,128)}), f32[64,2,16,1024]{3,2,0,1:T(8,128)}) %all-gather.5.cloned.1.call-update) | async-done | bytes 8388624 | tf_op jit(solution)/shard_map/all_gather | solution.py:11
  233.1 0.0 copy-start.5
  233.1 4.3 reduce_sum.55
  237.4 0.7 multiply_reduce_fusion.2
  238.1 139.1 %psum.43 = f32[]{:T(128)} all-reduce(f32[]{:T(128)} %get-tuple-element.14), channel_id=1, replica_groups=mesh['grid'=16,'mic'=4,'bin'=4] {'grid','bin'}, use_global_device_ids=true, to_apply=%region_2.0 | all-reduce | flops 1 | bytes 8 | tf_op jit(solution)/shard_map/psum | solution.py:50
  377.2 27.6 %psum.44 = f32[]{:T(128)} all-reduce(f32[]{:T(128)} %multiply_reduce_fusion.2), channel_id=1, replica_groups=mesh['grid'=16,'mic'=4,'bin'=4] {'mic','bin'}, use_global_device_ids=true, to_apply=%region_5.0 | all-reduce | flops 1 | bytes 8 | tf_op jit(solution)/shard_map/psum | solution.py:71
  406.1 0.0 copy-done.5
  406.1 0.1 fusion.10
  406.2 5.9 fusion.16
  412.2 0.0 copy-start.3
  412.2 6.0 fusion.17
  418.2 0.1 fusion.4
  418.3 0.8 pad_maximum_fusion.4
  419.1 0.0 all-reduce.5.cloned.1.call-update
  419.1 0.0 all-gather.7.cloned.1.call-start
  419.2 47.9 %all-reduce.5.cloned.1.call-done = f32[4,2,16,1024]{3,2,0,1:T(8,128)} async-done(((f32[4,2,16,1024]{3,2,0,1:T(8,128)}), f32[4,2,16,1024]{3,2,0,1:T(8,128)}) %all-reduce.5.cloned.1.call-update) | async-done | bytes 524304 | tf_op jit(solution)/shard_map/psum | solution.py:49
  467.1 1.8 multiply_reduce_fusion.1
  468.9 140.6 %psum.46 = f32[]{:T(128)} all-reduce(f32[]{:T(128)} %multiply_reduce_fusion.1), channel_id=1, replica_groups=mesh['grid'=16,'mic'=4,'bin'=4] {'grid','bin'}, use_global_device_ids=true, to_apply=%region_8.0 | all-reduce | flops 1 | bytes 8 | tf_op jit(solution)/shard_map/psum | solution.py:50
  610.7 0.0 copy-done.3
  610.7 1.1 fusion.9
  611.9 4.9 fusion.18
  616.8 4.9 fusion.19
  621.7 0.1 fusion.2
  621.8 0.8 pad_maximum_fusion.5
  622.6 0.0 all-gather.7.cloned.1.call-update
  622.6 73.5 %all-gather.7.cloned.1.call-done = f32[64,2,16,1024]{3,2,0,1:T(8,128)} async-done(((f32[4,2,16,1024]{3,2,0,1:T(8,128)}), f32[64,2,16,1024]{3,2,0,1:T(8,128)}) %all-gather.7.cloned.1.call-update) | async-done | bytes 8388624 | tf_op jit(solution)/shard_map/all_gather | solution.py:11
  696.2 0.0 copy-start.4
  696.2 4.3 reduce_sum.58
  700.5 0.7 multiply_reduce_fusion
  701.2 24.7 %psum.47 = f32[]{:T(128)} all-reduce(f32[]{:T(128)} %multiply_reduce_fusion), channel_id=1, replica_groups=mesh['grid'=16,'mic'=4,'bin'=4] {'mic','bin'}, use_global_device_ids=true, to_apply=%region_11.0 | all-reduce | flops 1 | bytes 8 | tf_op jit(solution)/shard_map/psum | solution.py:71
  727.1 0.1 multiply_subtract_fusion
  727.3 0.8 copy.14
  728.1 0.0 copy-done.4
  728.1 0.1 multiply_add_fusion
  728.2 0.8 copy.13
  (3 shorter events, 0.1 us)
Async XLA Ops:
  7.2 139.4 %all-reduce.3.cloned.1.call-start = ((), (), s32[]{:S(2)}) async-start(), calls=%async_computation | async-start | bytes 1048576 | tf_op jit(solution)/shard_map/psum | solution.py:49
  81.3 3.2 copy-start
  81.3 5.7 copy-start.2
  90.5 142.5 %all-gather.5.cloned.1.call-start = ((), (), s32[]{:S(2)}) async-start(), calls=%async_computation.2 | async-start | bytes 8912896 | tf_op jit(solution)/shard_map/all_gather | solution.py:11
  148.5 5.8 copy-start.1
  156.8 310.3 %all-reduce.5.cloned.1.call-start = ((), (), s32[]{:S(2)}) async-start(), calls=%async_computation.1 | async-start | bytes 1048576 | tf_op jit(solution)/shard_map/psum | solution.py:49
  233.1 173.0 %copy-start.5 = (f32[4,2,16,1024]{3,2,1,0:T(8,128)S(1)}, f32[4,2,16,1024]{3,2,1,0:T(8,128)}, u32[]{:S(2)}) copy-start(f32[4,2,16,1024]{3,2,1,0:T(8,128)} %param.7) | copy-start | bytes 1572868
  412.2 198.6 %copy-start.3 = (f32[4,2,16,1024]{3,2,0,1:T(8,128)S(1)}, f32[4,2,16,1024]{3,2,0,1:T(8,128)}, u32[]{:S(2)}) copy-start(f32[4,2,16,1024]{3,2,0,1:T(8,128)} %all-reduce.3.cloned.1.call-done) | copy-start | bytes 1572868
  419.1 277.1 %all-gather.7.cloned.1.call-start = ((), (), s32[]{:S(2)}) async-start(), calls=%async_computation.3 | async-start | bytes 8912896 | tf_op jit(solution)/shard_map/all_gather | solution.py:11
  696.2 31.9 %copy-start.4 = (f32[4,2,16,1024]{3,2,0,1:T(8,128)S(1)}, f32[4,2,16,1024]{3,2,0,1:T(8,128)}, u32[]{:S(2)}) copy-start(f32[4,2,16,1024]{3,2,0,1:T(8,128)} %all-reduce.5.cloned.1.call-done) | copy-start | bytes 1572868
Sparse Core Ops, SparseCore 0:
  90.7 55.8 all-reduce.2
  156.9 76.1 all-gather.4
  419.2 47.7 all-reduce.4
  622.8 73.3 all-gather.6
